TPU v7x, 32 devices: a whole 2x2x4 slice. The times are simulated.
32 devices in a mesh: groups: 2 (over y), width: 4 (over z), hidden: 2 (over x), batch: 2 (over core).
Axes of the slice: x: 2, y: 2, z: 4, core: 2. Of those that a mesh axis runs over, the one named last changes fastest.
Arguments:
- inputs: bfloat16 [2, 32, 16384], P(None, 'groups', 'width'), parts along dimension 1, may hold values from -42 to 42
- norm_gain: float32 [16384], P('width'), may hold values from 0.25 to 1.75
- wq_packed: int32 [16384, 4096], P('width', 'hidden'), may hold values from 0 to 255, as said below
- wq_scales: float32 [128, 8192], P('width', 'hidden'), may hold values from 0.002578125 to 0.01015625
- key_weight: bfloat16 [16384, 512], P('width', 'hidden'), may hold values from -0.046875 to 0.046875
- value_weight: bfloat16 [16384, 512], P('width', 'hidden'), may hold values from -0.046875 to 0.046875
- wo_weight: bfloat16 [8192, 16384], P('hidden', 'width'), may hold values from -0.3125 to 0.3125
- key_cache: bfloat16 [32, 1024, 512], P(('groups', 'width', 'batch'), None, 'hidden'), parts along dimension 0, may hold values from -6 to 6
- value_cache: bfloat16 [32, 1024, 512], P(('groups', 'width', 'batch'), None, 'hidden'), parts along dimension 0, may hold values from -6 to 6
- lengths: int32 [32], P(('groups', 'width', 'batch')), parts along dimension 0, may hold values from 256 to 1022, as said below
Outputs:
- attended: bfloat16 [2, 32, 16384], P(None, ('groups', 'hidden', 'batch'), 'width'), parts along dimension 1
There are 2 independent parts, one for each index of `groups`. A program takes and returns all parts, laid end to end along the dimension named above; an argument that names none is the same for every part. Nothing has to cross between parts.
Inputs may be any that keep to these rules, and one draw needn't show every extreme that they name: `wq_packed`: each word holds two 4-bit codes, bits 4 c to 4 c + 3 for column 2 j + c. `lengths`: some sequence has exactly 1022 filled slots.
All inputs are finite; a program needn't handle non-finite values.
Results may differ from a plain program's by a relative error of at most 0.0091.
Values may be sent and summed in bfloat16 or wider, within the bound.
No kernel may reach another device: no remote copies, remote signals or barrier semaphores. Data moves between devices by JAX's collectives and lax.ppermute only.
A program may use at most 448 MiB of HBM per device.

v0:
```python
import jax
import jax.numpy as jnp
from jax import lax
from jax.sharding import PartitionSpec as P

D = 16384
HEAD = 128
STEPS = 2


def unpack_weights(packed, scales, bits, per_word):
    shifts = jnp.arange(per_word, dtype=jnp.int32) * bits
    codes = packed[:, :, None] >> shifts & (1 << bits) - 1
    values = (codes - (1 << bits - 1)).astype(jnp.float32)
    values = values.reshape(packed.shape[0], packed.shape[1] * per_word)
    group_rows = packed.shape[0] // scales.shape[0]
    values = values.reshape(scales.shape[0], group_rows, values.shape[1]) * scales[:, None, :]
    return values.reshape(packed.shape[0], -1)


def rotate_heads(field, positions):
    half = field.shape[-1] // 2
    freq = 500000.0 ** (-2.0 * jnp.arange(half, dtype=jnp.float32) / field.shape[-1])
    angle = positions.astype(jnp.float32)[:, None] * freq[None, :]
    cosine = jnp.cos(angle)[:, None, :]
    sine = jnp.sin(angle)[:, None, :]
    first = field[..., :half]
    second = field[..., half:]
    return jnp.concatenate(
        [first * cosine - second * sine, second * cosine + first * sine], axis=-1
    )


def on_device(
    inputs,
    norm_gain,
    wq_packed,
    wq_scales,
    key_weight,
    value_weight,
    wo_weight,
    key_cache,
    value_cache,
    lengths,
):
    high = lax.Precision.HIGHEST
    w_query = unpack_weights(wq_packed, wq_scales, 4, 2)
    w_output = wo_weight.astype(jnp.float32)
    w_joined = jnp.concatenate(
        [w_query, key_weight.astype(jnp.float32), value_weight.astype(jnp.float32)], axis=1
    )
    seq_local = lengths.shape[0]
    slots = key_cache.shape[1]
    kv_local = key_weight.shape[1] // HEAD
    q_local = w_query.shape[1] // HEAD
    repeat = q_local // kv_local
    cols_local = inputs.shape[2]
    keys_all = key_cache
    values_all = value_cache
    slot_ids = jnp.arange(slots, dtype=jnp.int32)
    results = []
    for step in range(STEPS):
        rows = inputs[step].astype(jnp.float32)
        width_count = lax.axis_size("width")
        batch_count = lax.axis_size("batch")
        arranged = rows.reshape(width_count, batch_count, seq_local, cols_local)
        rows = lax.dynamic_index_in_dim(arranged, lax.axis_index("batch"), 1, keepdims=False)
        rows = rows.reshape(width_count * seq_local, cols_local)
        squares = jnp.sum(rows * rows, axis=1)
        total = lax.psum(squares, "width")
        scale = lax.rsqrt(total / D + 1e-05)
        normed = rows * scale[:, None] * norm_gain[None, :]
        partial_value = jnp.dot(
            normed, w_joined, precision=high, preferred_element_type=jnp.float32
        )
        terms = (partial_value,)
        summed = (lax.psum_scatter(terms[0], "width", scatter_dimension=0, tiled=True),)
        projected = summed[0]
        positions = lengths + step
        q_cols = q_local * HEAD
        kv_cols = kv_local * HEAD
        queries = rotate_heads(
            projected[:, :q_cols].reshape(seq_local, q_local, HEAD), positions
        ).astype(jnp.bfloat16)
        keys_new = rotate_heads(
            projected[:, q_cols : q_cols + kv_cols].reshape(seq_local, kv_local, HEAD), positions
        )
        keys_new = keys_new.reshape(seq_local, kv_cols).astype(jnp.bfloat16)
        values_new = projected[:, q_cols + kv_cols :].astype(jnp.bfloat16)
        written = slot_ids[None, :, None] == positions[:, None, None]
        keys_all = jnp.where(written, keys_new[:, None, :], keys_all)
        values_all = jnp.where(written, values_new[:, None, :], values_all)
        query_heads = queries.reshape(seq_local, kv_local, repeat, HEAD)
        key_heads = keys_all.reshape(seq_local, slots, kv_local, HEAD)
        value_heads = values_all.reshape(seq_local, slots, kv_local, HEAD)
        scores = jnp.einsum(
            "bgrd,bsgd->bgrs", query_heads, key_heads, preferred_element_type=jnp.float32
        ) * HEAD ** (-0.5)
        valid = slot_ids[None, None, None, :] <= positions[:, None, None, None]
        scores = jnp.where(valid, scores, -1e30)
        peak = jnp.max(scores, axis=-1, keepdims=True)
        weights = jnp.exp(scores - peak)
        total_weight = jnp.sum(weights, axis=-1, keepdims=True)
        probs = (weights / total_weight).astype(jnp.bfloat16)
        mixed = jnp.einsum(
            "bgrs,bsgd->bgrd", probs, value_heads, preferred_element_type=jnp.float32
        )
        mixed = mixed.reshape(seq_local, q_cols).astype(jnp.bfloat16)
        out_terms = jnp.dot(
            lax.all_gather(mixed, ("width", "batch"), axis=0, tiled=True).astype(jnp.float32),
            w_output,
            precision=high,
            preferred_element_type=jnp.float32,
        )
        head_sums = lax.psum_scatter(out_terms, "hidden", scatter_dimension=0, tiled=True)
        share = head_sums.shape[0] // lax.axis_size("batch")
        attended = lax.dynamic_slice_in_dim(head_sums, lax.axis_index("batch") * share, share, 0)
        results.append(attended.astype(jnp.bfloat16))
    return jnp.stack(results)


def solution(mesh):
    in_specs = (
        P(None, "groups", "width"),
        P("width"),
        P("width", "hidden"),
        P("width", "hidden"),
        P("width", "hidden"),
        P("width", "hidden"),
        P("hidden", "width"),
        P(("groups", "width", "batch"), None, "hidden"),
        P(("groups", "width", "batch"), None, "hidden"),
        P(("groups", "width", "batch")),
    )
    out_specs = P(None, ("groups", "hidden", "batch"), "width")
    return jax.shard_map(
        on_device, mesh=mesh, in_specs=in_specs, out_specs=out_specs, check_vma=False
    )
```

profile of v0, /device:TPU:0, one launch (start us, length us, event | category | flops | bytes accessed | tf_op | source)
XLA Modules:
  0.0 575.9 jit_solution(8795833345152713637)
XLA Ops:
  6.5 1.0 slice_convert_fusion.1
  7.5 0.2 reshape.291
  7.7 0.2 reshape.292
  7.9 0.2 multiply_reduce_fusion
  8.1 0.1 reduce_sum.41
  8.2 0.1 reduce_sum.44
  8.2 13.4 %all-reduce.2 = (f32[8]{0:T(128)S(1)}, f32[8]{0:T(128)S(1)}) all-reduce(f32[8]{0:T(128)S(1)} %reduce_sum.44, f32[8]{0:T(128)S(1)} %reduce_sum.41), channel_id=1, replica_groups=mesh['groups'=2,'width'=4,'hidden'=2,'batch'=2] {'width'}, use_global_device_ids=true, to_apply=%region_7.8 | all-reduce | flops 16 | bytes 128 | tf_op jit(solution)/shard_map/psum | solution.py:70
  21.7 0.5 add_rsqrt_fusion.1
  22.2 0.7 reshape.281
  22.9 31.1 %copy.23 = s32[4096,2048]{0,1:T(8,128)} copy(s32[4096,2048]{1,0:T(8,128)} %param.12) | data formatting | bytes 67108864 | tf_op args[2]
  54.0 39.8 %shift_right_arithmetic.21 = s32[4096,2048,2]{0,2,1:T(2,128)} broadcast(s32[4096,2048]{0,1:T(8,128)} %copy.23), dimensions={0,1} | broadcast | bytes 100663296 | tf_op jit(solution)/shard_map/shift_right_arithmetic | solution.py:13
  93.8 78.3 %shift_right_arithmetic.22 = s32[4096,4096]{0,1:T(8,128)} reshape(s32[4096,2048,2]{0,2,1:T(2,128)} %shift_right_arithmetic.21) | data formatting | bytes 134217728 | tf_op jit(solution)/shard_map/shift_right_arithmetic | solution.py:13
  172.1 0.6 copy.24
  172.7 0.1 shift_right_arithmetic.23
  172.8 0.5 shift_right_arithmetic.24
  173.3 4.1 copy.25
  177.4 4.0 convert_element_type.85
  181.4 4.1 copy.26
  185.5 4.1 convert_element_type.86
  189.6 0.1 reshape.286
  189.7 41.1 %mul.120 = f32[32,128,4096]{1,0,2:T(8,128)} broadcast(f32[32,4096]{0,1:T(8,128)S(1)} %copy.24), dimensions={0,2} | broadcast | bytes 67633152 | tf_op jit(solution)/shard_map/mul | solution.py:17
  230.7 79.0 %bitcast_multiply_fusion = f32[4096,4096]{0,1:T(8,128)} fusion(f32[512,8,32,128]{3,2,1,0:T(8,128)} %bitcast.17, s32[4096,4096]{0,1:T(8,128)} %shift_right_arithmetic.22, s32[4096]{0:T(1024)S(1)} %shift_right_arithmetic.24), kind=kLoop, calls=%fused_computation.3 | loop fusion | flops 83886080 | bytes 201342976 | tf_op jit(solution)/shard_map/mul | solution.py:17
  309.8 78.8 %fusion.3 = f32[8,4608]{1,0:T(8,128)} fusion(f32[4096,256]{0,1:T(8,128)} %convert_element_type.86, f32[4096,256]{0,1:T(8,128)} %convert_element_type.85, f32[4096,4096]{0,1:T(8,128)} %bitcast_multiply_fusion, f32[8,4096]{1,0:T(8,128)S(1)} %copy-done.5, f32[4096]{0:T(1024)S(1)} %copy-done.7, f32[8]{0:T(128)S(1)} %copy-done.9), kind=kOutput, calls=%fused_computation.5 | convolution fusion | flops 1849753600 | bytes 75792416 | tf_op jit(solution)/shard_map/dot_general | solution.py:73
  388.5 0.0 copy-start.8
  388.6 65.2 %fusion.2 = f32[8,4608]{1,0:T(8,128)} fusion(f32[4096,256]{0,1:T(8,128)S(1)} %copy-done.1, f32[4096,256]{0,1:T(8,128)S(1)} %copy-done, f32[4096,4096]{0,1:T(8,128)} %bitcast_multiply_fusion, f32[8,4096]{1,0:T(8,128)S(1)} %reshape.286, f32[8]{0:T(128)S(1)} %add_rsqrt_fusion, f32[4096]{0:T(1024)S(1)} %copy-done.7), kind=kOutput, calls=%fused_computation.4 | convolution fusion | flops 1849753600 | bytes 75792416 | tf_op jit(solution)/shard_map/dot_general | solution.py:73
  453.8 0.0 all-reduce.6.cloned.1.call-update
  453.8 0.0 reduce-scatter.3.cloned.1.call-start
  453.9 0.1 multiply_cosine_fusion.1
  454.1 0.6 dynamic-slice
  455.3 0.1 iota_compare_fusion.1
  455.4 32.9 %all-reduce.6.cloned.1.call-done = (f32[8,4608]{1,0:T(8,128)}, f32[8,4608]{1,0:T(8,128)}) async-done(((f32[8,4608]{1,0:T(8,128)}, f32[8,4608]{1,0:T(8,128)}), (f32[8,4608]{1,0:T(8,128)}, f32[8,4608]{1,0:T(8,128)})) %all-reduce.6.cloned.1.call-update) | async-done | bytes 294928
  488.3 0.8 dynamic-slice.8
  489.0 0.8 dynamic-slice.5
  489.8 0.8 dynamic-slice.14
  490.6 0.8 dynamic-slice.15
  491.4 0.9 dynamic-slice_bitcast_fusion.1
  492.3 0.9 dynamic-slice_bitcast_fusion
  493.2 0.1 subtract_convert_fusion.2
  493.3 0.1 maximum_bitcast_fusion.1
  493.4 0.1 subtract_convert_fusion.3
  493.5 0.1 maximum_bitcast_fusion
  493.6 0.1 subtract_convert_fusion.1
  493.7 2.4 fusion.19
  496.1 0.4 fusion.8
  496.5 0.2 fusion.47
  496.7 1.6 convolution_convert_fusion.1
  498.3 14.0 %all-gather = bf16[8,2,4096]{2,1,0:T(2,128)(2,1)S(1)} all-gather(bf16[1,2,4096]{2,1,0:T(2,128)(2,1)S(1)} %reshape.293), channel_id=1, replica_groups=mesh['groups'=2,'width'=4,'hidden'=2,'batch'=2] {'width','batch'}, dimensions={0}, use_global_device_ids=true | all-gather | bytes 147456 | tf_op jit(solution)/shard_map/all_gather | solution.py:110
  512.3 0.1 reshape.294
  512.3 13.8 %fusion.48 = f32[16,4096]{1,0:T(8,128)} fusion(bf16[16,4096]{1,0:T(8,128)(2,1)S(1)} %reshape.294, bf16[4096,4096]{1,0:T(8,128)(2,1)} %param.16), kind=kOutput, calls=%fused_computation.100 | convolution fusion | flops 536870912 | bytes 33947648 | tf_op jit(solution)/shard_map/dot_general | solution.py:109
  526.1 0.0 reduce-scatter.3.cloned.1.call-update
  526.1 0.0 reduce-scatter.5.cloned.1.call-start
  526.2 0.1 subtract_convert_fusion
  526.3 0.4 fusion.9
  526.7 0.2 fusion.46
  526.9 1.6 convolution_convert_fusion
  528.5 14.0 %all-gather.1 = bf16[8,2,4096]{2,1,0:T(2,128)(2,1)S(1)} all-gather(bf16[1,2,4096]{2,1,0:T(2,128)(2,1)S(1)} %reshape.295), channel_id=1, replica_groups=mesh['groups'=2,'width'=4,'hidden'=2,'batch'=2] {'width','batch'}, dimensions={0}, use_global_device_ids=true | all-gather | bytes 147456 | tf_op jit(solution)/shard_map/all_gather | solution.py:110
  542.5 0.1 reshape.296
  542.5 13.5 %fusion.49 = f32[16,4096]{1,0:T(8,128)} fusion(bf16[16,4096]{1,0:T(8,128)(2,1)S(1)} %reshape.296, bf16[4096,4096]{1,0:T(8,128)(2,1)} %param.16), kind=kOutput, calls=%fused_computation.101 | convolution fusion | flops 536870912 | bytes 33947648 | tf_op jit(solution)/shard_map/dot_general | solution.py:109
  556.1 0.0 reduce-scatter.5.cloned.1.call-update
  556.1 0.0 reduce-scatter.3.cloned.1.call-done
  556.1 0.9 fusion.30
  557.1 10.7 %reduce-scatter.5.cloned.1.call-done = f32[8,4096]{1,0:T(8,128)} async-done(((f32[16,4096]{1,0:T(8,128)}), f32[8,4096]{1,0:T(8,128)}) %reduce-scatter.5.cloned.1.call-update) | async-done | bytes 131088 | tf_op jit(solution)/shard_map/reduce_scatter | solution.py:115
  567.7 0.9 fusion.31
  568.7 0.7 pad_maximum_fusion.3
  (32 shorter events, 0.2 us)
Async XLA Ops:
  6.5 481.7 %all-reduce.6.cloned.1.call-start = ((), (), s32[]{:S(2)}) async-start(), calls=%async_computation.4 | async-start | bytes 589824
  93.8 78.3 %copy-start.4 = (f32[32,4096]{1,0:T(8,128)S(1)}, f32[32,4096]{1,0:T(8,128)}, u32[]{:S(2)}) copy-start(f32[32,4096]{1,0:T(8,128)} %param.13) | copy-start | bytes 1572868
  230.7 79.0 %copy-start.5 = (f32[8,4096]{1,0:T(8,128)S(1)}, f32[8,4096]{1,0:T(8,128)}, u32[]{:S(2)}) copy-start(f32[8,4096]{1,0:T(8,128)} %reshape.281) | copy-start | bytes 393220
  230.7 79.0 %copy-start.7 = (f32[4096]{0:T(1024)S(1)}, f32[4096]{0:T(1024)}, u32[]{:S(2)}) copy-start(f32[4096]{0:T(1024)} %param.11) | copy-start | bytes 49156
  230.7 79.0 %copy-start.9 = (f32[8]{0:T(128)S(1)}, f32[8]{0:T(128)}, u32[]{:S(2)}) copy-start(f32[8]{0:T(128)} %add_rsqrt_fusion.1) | copy-start | bytes 100
  309.8 78.8 %copy-start = (f32[4096,256]{0,1:T(8,128)S(1)}, f32[4096,256]{0,1:T(8,128)}, u32[]{:S(2)}) copy-start(f32[4096,256]{0,1:T(8,128)} %convert_element_type.85) | copy-start | bytes 12582916
  309.8 78.8 %copy-start.1 = (f32[4096,256]{0,1:T(8,128)S(1)}, f32[4096,256]{0,1:T(8,128)}, u32[]{:S(2)}) copy-start(f32[4096,256]{0,1:T(8,128)} %convert_element_type.86) | copy-start | bytes 12582916
  388.5 65.4 %copy-start.6 = (s32[2]{0:T(128)S(1)}, s32[2]{0:T(128)}, u32[]{:S(2)}) copy-start(s32[2]{0:T(128)} %param.19) | copy-start | bytes 28
  388.5 65.5 %copy-start.8 = (u32[32]{0:T(128)S(1)}, u32[32]{0:T(128)}, u32[]{:S(2)}) copy-start(u32[32]{0:T(128)} %constant.51) | copy-start | bytes 388
  388.5 105.1 %copy-start.2 = (bf16[2,1024,256]{2,1,0:T(8,128)(2,1)S(1)}, bf16[2,1024,256]{2,1,0:T(8,128)(2,1)}, u32[]{:S(2)}) copy-start(bf16[2,1024,256]{2,1,0:T(8,128)(2,1)} %param.18) | copy-start | bytes 3145732
  388.6 105.1 %copy-start.3 = (bf16[2,1024,256]{2,1,0:T(8,128)(2,1)S(1)}, bf16[2,1024,256]{2,1,0:T(8,128)(2,1)}, u32[]{:S(2)}) copy-start(bf16[2,1024,256]{2,1,0:T(8,128)(2,1)} %param.17) | copy-start | bytes 3145732
  453.8 102.3 %reduce-scatter.3.cloned.1.call-start = ((), (), s32[]{:S(2)}) async-start(), calls=%async_computation.2 | async-start | bytes 393216 | tf_op jit(solution)/shard_map/reduce_scatter | solution.py:115
  526.1 41.6 %reduce-scatter.5.cloned.1.call-start = ((), (), s32[]{:S(2)}) async-start(), calls=%async_computation.3 | async-start | bytes 393216 | tf_op jit(solution)/shard_map/reduce_scatter | solution.py:115
Sparse Core Ops, SparseCore 0:
  454.0 34.2 all-reduce.5
  526.3 11.4 reduce-scatter.2
  556.2 11.4 reduce-scatter.4
where the time goes:
time: 579 us; the launch traced here: 576 us
  local copies, waits for them, and re-layouts  209 us (36%)
  matrix products  175 us (30%)
  other arithmetic  93 us (16%)
  waiting for transfers between devices  43.6 us (8%)
  blocking collectives  41.4 us (7%)
  between operations  14 us (2%)
    dot_general x2, matrix products, on_device(): jnp.dot(normed, w_joined, precision=high, preferred_element_type=jnp.floa...  144 us
    shift_right_arithmetic x4, local copies, waits for them, and re-layouts, unpack_weights(): codes = packed[:, :, None] >> shifts & (1 << bits) - 1  119 us
    mul x1, other arithmetic, unpack_weights(): values.reshape(scales.shape[0], group_rows, values.shape[1])  79 us
    unnamed x35, local copies, waits for them, and re-layouts  42.6 us
    mul x1, local copies, waits for them, and re-layouts, unpack_weights(): values.reshape(scales.shape[0], group_rows, values.shape[1])  41.1 us
    unnamed x4, waiting for transfers between devices  32.9 us
    all_gather x2, blocking collectives, on_device(): lax.all_gather(mixed, ('width', 'batch'), axis=0, tiled=True)  28 us
    dot_general x2, matrix products, on_device(): jnp.dot(lax.all_gather(mixed, ('width', 'batch'), axis=0, tiled=True).ast...  27.3 us
  transfers between devices with their start and end apart: 3, of which 2 were waited for; matrix products, arithmetic and copies ran while one was open for 3% of the time, Pallas kernels for 0%

commit v1 on v0

--- a/solution.py
+++ b/solution.py
@@ -6,6 +6,17 @@
 D = 16384
 HEAD = 128
 STEPS = 2
+
+
+def refer_sites(original):
+    num_devices = jax.lax.axis_size("width")
+    odd = original
+    for d in [
+        [(h, h ^ w) for h in range(num_devices)] for w in (1, 2, 4, 8, 16) if w < num_devices
+    ]:
+        tmp = jax.lax.ppermute(odd, axis_name="width", perm=d)
+        odd = odd + tmp
+    return odd
 
 
 def unpack_weights(packed, scales, bits, per_word):
@@ -67,7 +78,7 @@
         rows = lax.dynamic_index_in_dim(arranged, lax.axis_index("batch"), 1, keepdims=False)
         rows = rows.reshape(width_count * seq_local, cols_local)
         squares = jnp.sum(rows * rows, axis=1)
-        total = lax.psum(squares, "width")
+        total = refer_sites(squares)
         scale = lax.rsqrt(total / D + 1e-05)
         normed = rows * scale[:, None] * norm_gain[None, :]
         partial_value = jnp.dot(

time: 579 us -> 578 us (level)
  blocking collectives: 41.4 us -> 28 us
  starting transfers between devices: 0.09 us -> 6.57 us
    psum x1 -> x0, blocking collectives: 13.4 us -> none  [on_device(): total = lax.psum(squares, 'width')]
    ppermute x0 -> x4, starting transfers between devices: none -> 6.49 us  [refer_sites(): tmp = jax.lax.ppermute(odd, axis_name='width', perm=d)]
  transfers between devices with their start and end apart: 3 -> 7, of which waited for: 2 -> 3; matrix products, arithmetic and copies ran while one was open for 3% -> 67% of each run, Pallas kernels for 0% -> 0%
where the time goes in v1:
time: 578 us; the launch traced here: 575 us
  local copies, waits for them, and re-layouts  210 us (36%)
  matrix products  175 us (30%)
  other arithmetic  94.5 us (16%)
  waiting for transfers between devices  47.4 us (8%)
  blocking collectives  28 us (5%)
  between operations  14 us (2%)
  starting transfers between devices  6.57 us (1%)
    dot_general x2, matrix products, on_device(): jnp.dot(normed, w_joined, precision=high, preferred_element_type=jnp.floa...  144 us
    shift_right_arithmetic x4, local copies, waits for them, and re-layouts, unpack_weights(): codes = packed[:, :, None] >> shifts & (1 << bits) - 1  119 us
    mul x1, other arithmetic, unpack_weights(): values.reshape(scales.shape[0], group_rows, values.shape[1])  79 us
    unnamed x35, local copies, waits for them, and re-layouts  42.6 us
    mul x1, local copies, waits for them, and re-layouts, unpack_weights(): values.reshape(scales.shape[0], group_rows, values.shape[1])  41 us
    unnamed x4, waiting for transfers between devices  36.3 us
    all_gather x2, blocking collectives, on_device(): lax.all_gather(mixed, ('width', 'batch'), axis=0, tiled=True)  28 us
    dot_general x2, matrix products, on_device(): jnp.dot(lax.all_gather(mixed, ('width', 'batch'), axis=0, tiled=True).ast...  27.3 us
  transfers between devices with their start and end apart: 7, of which 3 were waited for; matrix products, arithmetic and copies ran while one was open for 67% of the time, Pallas kernels for 0%

profile of v1, /device:TPU:0, one launch (start us, length us, event | category | flops | bytes accessed | tf_op | source)
XLA Modules:
  0.0 575.1 jit_solution(14285009847147021850)
XLA Ops:
  6.5 1.0 slice_convert_fusion.1
  7.5 0.2 reshape.291
  7.7 0.2 reshape.292
  7.9 0.2 multiply_reduce_fusion
  8.1 0.6 reduce_sum.41
  8.7 3.0 collective-permute-start
  11.7 0.6 reduce_sum.44
  12.3 0.6 multiply_power_fusion
  12.9 0.7 reshape.281
  13.6 31.2 %copy.23 = s32[4096,2048]{0,1:T(8,128)} copy(s32[4096,2048]{1,0:T(8,128)} %param.12) | data formatting | bytes 67108864 | tf_op args[2]
  44.8 39.8 %shift_right_arithmetic.21 = s32[4096,2048,2]{0,2,1:T(2,128)} broadcast(s32[4096,2048]{0,1:T(8,128)} %copy.23), dimensions={0,1} | broadcast | bytes 100663296 | tf_op jit(solution)/shard_map/shift_right_arithmetic | solution.py:24
  84.6 78.3 %shift_right_arithmetic.22 = s32[4096,4096]{0,1:T(8,128)} reshape(s32[4096,2048,2]{0,2,1:T(2,128)} %shift_right_arithmetic.21) | data formatting | bytes 134217728 | tf_op jit(solution)/shard_map/shift_right_arithmetic | solution.py:24
  162.9 0.6 copy.24
  163.5 0.1 shift_right_arithmetic.23
  163.6 0.5 shift_right_arithmetic.24
  164.0 4.1 copy.25
  168.1 4.0 convert_element_type.85
  172.2 4.1 copy.26
  176.3 4.0 convert_element_type.86
  180.3 0.1 reshape.286
  180.4 41.0 %mul.120 = f32[32,128,4096]{1,0,2:T(8,128)} broadcast(f32[32,4096]{0,1:T(8,128)S(1)} %copy.24), dimensions={0,2} | broadcast | bytes 67633152 | tf_op jit(solution)/shard_map/mul | solution.py:28
  221.5 79.0 %bitcast_multiply_fusion = f32[4096,4096]{0,1:T(8,128)} fusion(f32[512,8,32,128]{3,2,1,0:T(8,128)} %bitcast.17, s32[4096,4096]{0,1:T(8,128)} %shift_right_arithmetic.22, s32[4096]{0:T(1024)S(1)} %shift_right_arithmetic.24), kind=kLoop, calls=%fused_computation.3 | loop fusion | flops 83886080 | bytes 201342976 | tf_op jit(solution)/shard_map/mul | solution.py:28
  300.5 0.8 add.54
  301.3 3.1 collective-permute-start.1
  304.4 0.7 add.61
  305.1 0.4 collective-permute-start.3
  305.5 0.4 collective-permute-done.1
  305.9 78.6 %fusion.3 = f32[8,4608]{1,0:T(8,128)} fusion(f32[4096,256]{0,1:T(8,128)} %convert_element_type.86, f32[4096,256]{0,1:T(8,128)} %convert_element_type.85, f32[4096,4096]{0,1:T(8,128)} %bitcast_multiply_fusion, f32[8,4096]{1,0:T(8,128)S(1)} %copy-done.5, f32[4096]{0:T(1024)S(1)} %copy-done.8, f32[8]{0:T(128)S(1)} %add_rsqrt_fusion.1), kind=kOutput, calls=%fused_computation.5 | convolution fusion | flops 1849753600 | bytes 75792416 | tf_op jit(solution)/shard_map/dot_general | solution.py:84
  384.6 65.2 %fusion.2 = f32[8,4608]{1,0:T(8,128)} fusion(f32[4096,256]{0,1:T(8,128)S(1)} %copy-done.1, f32[4096,256]{0,1:T(8,128)S(1)} %copy-done, f32[4096,4096]{0,1:T(8,128)} %bitcast_multiply_fusion, f32[8,4096]{1,0:T(8,128)S(1)} %reshape.286, f32[8]{0:T(128)S(1)} %add_rsqrt_fusion, f32[4096]{0:T(1024)S(1)} %copy-done.8), kind=kOutput, calls=%fused_computation.4 | convolution fusion | flops 1849753600 | bytes 75792416 | tf_op jit(solution)/shard_map/dot_general | solution.py:84
  449.8 0.0 reduce-scatter.3.cloned.1.call-start
  449.9 0.1 multiply_cosine_fusion.1
  450.0 0.6 dynamic-slice
  451.3 0.1 iota_compare_fusion.1
  451.4 36.3 %all-reduce.5.cloned.1.call-done = (f32[8,4608]{1,0:T(8,128)}, f32[8,4608]{1,0:T(8,128)}) async-done(((f32[8,4608]{1,0:T(8,128)}, f32[8,4608]{1,0:T(8,128)}), (f32[8,4608]{1,0:T(8,128)}, f32[8,4608]{1,0:T(8,128)})) %all-reduce.5.cloned.1.call-update) | async-done | bytes 294928
  487.6 0.8 dynamic-slice.8
  488.4 0.8 dynamic-slice.5
  489.2 0.8 dynamic-slice.14
  489.9 0.8 dynamic-slice.15
  490.7 0.9 dynamic-slice_bitcast_fusion.1
  491.6 0.9 dynamic-slice_bitcast_fusion
  492.6 0.1 subtract_convert_fusion.2
  492.7 0.1 maximum_bitcast_fusion.1
  492.8 0.1 subtract_convert_fusion.3
  492.8 0.1 maximum_bitcast_fusion
  492.9 0.1 subtract_convert_fusion.1
  493.1 2.4 fusion.19
  495.4 0.4 fusion.8
  495.8 0.2 fusion.47
  496.0 1.6 convolution_convert_fusion.1
  497.6 14.0 %all-gather = bf16[8,2,4096]{2,1,0:T(2,128)(2,1)S(1)} all-gather(bf16[1,2,4096]{2,1,0:T(2,128)(2,1)S(1)} %reshape.293), channel_id=1, replica_groups=mesh['groups'=2,'width'=4,'hidden'=2,'batch'=2] {'width','batch'}, dimensions={0}, use_global_device_ids=true | all-gather | bytes 147456 | tf_op jit(solution)/shard_map/all_gather | solution.py:121
  511.6 0.1 reshape.294
  511.6 13.8 %fusion.48 = f32[16,4096]{1,0:T(8,128)} fusion(bf16[16,4096]{1,0:T(8,128)(2,1)S(1)} %reshape.294, bf16[4096,4096]{1,0:T(8,128)(2,1)} %param.16), kind=kOutput, calls=%fused_computation.100 | convolution fusion | flops 536870912 | bytes 33947648 | tf_op jit(solution)/shard_map/dot_general | solution.py:120
  525.4 0.0 reduce-scatter.5.cloned.1.call-start
  525.5 0.1 subtract_convert_fusion
  525.6 0.4 fusion.9
  526.0 0.2 fusion.46
  526.2 1.6 convolution_convert_fusion
  527.8 14.0 %all-gather.1 = bf16[8,2,4096]{2,1,0:T(2,128)(2,1)S(1)} all-gather(bf16[1,2,4096]{2,1,0:T(2,128)(2,1)S(1)} %reshape.295), channel_id=1, replica_groups=mesh['groups'=2,'width'=4,'hidden'=2,'batch'=2] {'width','batch'}, dimensions={0}, use_global_device_ids=true | all-gather | bytes 147456 | tf_op jit(solution)/shard_map/all_gather | solution.py:121
  541.8 0.1 reshape.296
  541.8 13.5 %fusion.49 = f32[16,4096]{1,0:T(8,128)} fusion(bf16[16,4096]{1,0:T(8,128)(2,1)S(1)} %reshape.296, bf16[4096,4096]{1,0:T(8,128)(2,1)} %param.16), kind=kOutput, calls=%fused_computation.101 | convolution fusion | flops 536870912 | bytes 33947648 | tf_op jit(solution)/shard_map/dot_general | solution.py:120
  555.4 0.9 fusion.30
  556.3 10.7 %reduce-scatter.5.cloned.1.call-done = f32[8,4096]{1,0:T(8,128)} async-done(((f32[16,4096]{1,0:T(8,128)}), f32[8,4096]{1,0:T(8,128)}) %reduce-scatter.5.cloned.1.call-update) | async-done | bytes 131088 | tf_op jit(solution)/shard_map/reduce_scatter | solution.py:126
  567.0 0.9 fusion.31
  567.9 0.7 pad_maximum_fusion.3
  (41 shorter events, 0.2 us)
Async XLA Ops:
  6.5 481.1 %all-reduce.5.cloned.1.call-start = ((), (), s32[]{:S(2)}) async-start(), calls=%async_computation.4 | async-start | bytes 589824
  8.7 291.8 %collective-permute-start = (f32[8]{0:T(128)}, f32[8]{0:T(128)}, u32[]{:S(2)}, u32[]{:S(2)}) collective-permute-start(f32[8]{0:T(128)} %reduce_sum.41), channel_id=1, source_target_pairs={{0,4},{4,0},{8,12},{12,8},{1,5},{5,1},{9,13},{13,9},{2,6},{6,2},{1... | collective-permute-start | bytes 104 | tf_op jit(solution)/shard_map/ppermute | solution.py:17
  12.3 292.1 %collective-permute-start.2 = (f32[8]{0:T(128)}, f32[8]{0:T(128)}, u32[]{:S(2)}, u32[]{:S(2)}) collective-permute-start(f32[8]{0:T(128)} %reduce_sum.44), channel_id=1, source_target_pairs={{0,4},{4,0},{8,12},{12,8},{1,5},{5,1},{9,13},{13,9},{2,6},{6,2},{1... | collective-permute-start | bytes 104 | tf_op jit(solution)/shard_map/ppermute | solution.py:17
  84.5 78.3 %copy-start.4 = (f32[32,4096]{1,0:T(8,128)S(1)}, f32[32,4096]{1,0:T(8,128)}, u32[]{:S(2)}) copy-start(f32[32,4096]{1,0:T(8,128)} %param.13) | copy-start | bytes 1572868
  84.5 95.9 %copy-start.6 = (s32[2]{0:T(128)S(1)}, s32[2]{0:T(128)}, u32[]{:S(2)}) copy-start(s32[2]{0:T(128)} %param.19) | copy-start | bytes 28
  221.5 84.4 %copy-start.5 = (f32[8,4096]{1,0:T(8,128)S(1)}, f32[8,4096]{1,0:T(8,128)}, u32[]{:S(2)}) copy-start(f32[8,4096]{1,0:T(8,128)} %reshape.281) | copy-start | bytes 393220
  221.5 84.4 %copy-start.8 = (f32[4096]{0:T(1024)S(1)}, f32[4096]{0:T(1024)}, u32[]{:S(2)}) copy-start(f32[4096]{0:T(1024)} %param.11) | copy-start | bytes 49156
  300.5 84.1 %copy-start = (f32[4096,256]{0,1:T(8,128)S(1)}, f32[4096,256]{0,1:T(8,128)}, u32[]{:S(2)}) copy-start(f32[4096,256]{0,1:T(8,128)} %convert_element_type.85) | copy-start | bytes 12582916
  300.5 84.1 %copy-start.1 = (f32[4096,256]{0,1:T(8,128)S(1)}, f32[4096,256]{0,1:T(8,128)}, u32[]{:S(2)}) copy-start(f32[4096,256]{0,1:T(8,128)} %convert_element_type.86) | copy-start | bytes 12582916
  301.3 4.6 collective-permute-start.1
  305.1 79.4 %collective-permute-start.3 = (f32[8]{0:T(128)S(1)}, f32[8]{0:T(128)S(1)}, u32[]{:S(2)}, u32[]{:S(2)}) collective-permute-start(f32[8]{0:T(128)S(1)} %add.61), channel_id=1, source_target_pairs={{0,8},{4,12},{8,0},{12,4},{1,9},{5,13},{9,1},{13,5},{2,10},{6,14},... | collective-permute-start | bytes 104 | tf_op jit(solution)/shard_map/ppermute | solution.py:17
  384.5 65.4 %copy-start.7 = (f32[64]{0:T(128)S(1)}, f32[64]{0:T(128)}, u32[]{:S(2)}) copy-start(f32[64]{0:T(128)} %multiply_power_fusion) | copy-start | bytes 772
  384.5 65.5 %copy-start.9 = (u32[32]{0:T(128)S(1)}, u32[32]{0:T(128)}, u32[]{:S(2)}) copy-start(u32[32]{0:T(128)} %constant.51) | copy-start | bytes 388
  384.5 108.5 %copy-start.2 = (bf16[2,1024,256]{2,1,0:T(8,128)(2,1)S(1)}, bf16[2,1024,256]{2,1,0:T(8,128)(2,1)}, u32[]{:S(2)}) copy-start(bf16[2,1024,256]{2,1,0:T(8,128)(2,1)} %param.18) | copy-start | bytes 3145732
  384.5 108.5 %copy-start.3 = (bf16[2,1024,256]{2,1,0:T(8,128)(2,1)S(1)}, bf16[2,1024,256]{2,1,0:T(8,128)(2,1)}, u32[]{:S(2)}) copy-start(bf16[2,1024,256]{2,1,0:T(8,128)(2,1)} %param.17) | copy-start | bytes 3145732
  449.8 105.6 %reduce-scatter.3.cloned.1.call-start = ((), (), s32[]{:S(2)}) async-start(), calls=%async_computation.2 | async-start | bytes 393216 | tf_op jit(solution)/shard_map/reduce_scatter | solution.py:126
  525.4 41.6 %reduce-scatter.5.cloned.1.call-start = ((), (), s32[]{:S(2)}) async-start(), calls=%async_computation.3 | async-start | bytes 393216 | tf_op jit(solution)/shard_map/reduce_scatter | solution.py:126
Sparse Core Ops, SparseCore 0:
  449.9 37.6 all-reduce.4
  525.6 11.4 reduce-scatter.2
  555.5 11.4 reduce-scatter.4
